TPU v7x, 32 devices: a whole 2x2x4 slice. The times are simulated.
32 devices in a mesh: grp: 2 (over y), seq: 4 (over z), head: 2 (over x), sub: 2 (over core).
Axes of the slice: x: 2, y: 2, z: 4, core: 2. Of those that a mesh axis runs over, the one named last changes fastest.
Arguments:
- vid_q: bfloat16 [2560, 4096], P(('grp', 'seq', 'sub'), 'head'), parts along dimension 0, may hold values from -6 to 6
- vid_k: bfloat16 [2560, 4096], P(('grp', 'seq', 'sub'), 'head'), parts along dimension 0, may hold values from -6 to 6
- vid_v: bfloat16 [2560, 4096], P(('grp', 'seq', 'sub'), 'head'), parts along dimension 0, may hold values from -6 to 6
- aud_q: bfloat16 [640, 2048], P(('grp', 'seq', 'sub'), 'head'), parts along dimension 0, may hold values from -6 to 6
- cross_k: bfloat16 [2560, 2048], P(('grp', 'seq', 'sub'), 'head'), parts along dimension 0, may hold values from -6 to 6
- cross_v: bfloat16 [2560, 2048], P(('grp', 'seq', 'sub'), 'head'), parts along dimension 0, may hold values from -6 to 6
- cross_q: bfloat16 [2560, 2048], P(('grp', 'seq', 'sub'), 'head'), parts along dimension 0, may hold values from -6 to 6
- aud_k: bfloat16 [640, 2048], P(('grp', 'seq', 'sub'), 'head'), parts along dimension 0, may hold values from -6 to 6
- aud_v: bfloat16 [640, 2048], P(('grp', 'seq', 'sub'), 'head'), parts along dimension 0, may hold values from -6 to 6
- windows: int32 [2, 80], P(None, 'grp'), parts along dimension 1, may hold values from 0 to 40, as said below
Outputs:
- video_self: bfloat16 [2560, 4096], P(('grp', 'seq', 'sub'), 'head'), parts along dimension 0
- audio_out: bfloat16 [640, 2048], P(('grp', 'seq', 'sub'), 'head'), parts along dimension 0
- video_cross: bfloat16 [2560, 2048], P(('grp', 'seq', 'sub'), 'head'), parts along dimension 0
There are 2 independent parts, one for each index of `grp`. A program takes and returns all parts, laid end to end along the dimension named above; each array names one. Nothing has to cross between parts.
Inputs may be any that keep to these rules, and one draw needn't show every extreme that they name: For every stretch c, windows[0, c] lies between max(0, c - 5) and c, and windows[1, c] between c + 1 and min(40, c + 6); in every draw some stretch reaches 5 tiles on both sides.
All inputs are finite; a program needn't handle non-finite values.
Results may differ from a plain program's by a relative error of at most 0.03.
Values may be sent and summed in bfloat16 or wider, within the bound.
A program may use at most 64 MiB of HBM per device.

v0:
```python
from functools import partial
import math

import jax
import jax.numpy as jnp
from jax import lax
from jax.sharding import PartitionSpec as P

HEAD_DIM = 128
AUDIO_DIM = 64
TILE_LEN = 32
STRETCH_LEN = 8


def extended(cells, sides, width):
    for axis, dim in sides:
        count = lax.axis_size(axis)
        ends = count - 1
        head = lax.slice_in_dim(cells, 0, width, axis=dim)
        tail = lax.slice_in_dim(cells, cells.shape[dim] - width, cells.shape[dim], axis=dim)
        cells = jnp.concatenate(
            [
                lax.ppermute(tail, axis, [(i, (i + 1) % count) for i in range(ends)]),
                cells,
                lax.ppermute(head, axis, [((i + 1) % count, i) for i in range(ends)]),
            ],
            axis=dim,
        )
    return cells


def start_state(query_count, head_count, head_size):
    running = jnp.full((head_count, query_count), -jnp.inf, jnp.float32)
    summed = jnp.zeros((head_count, query_count), jnp.float32)
    numerator = jnp.zeros((head_count, query_count, head_size), jnp.float32)
    return (running, summed, numerator)


def absorb(state_in, queries, key_rows, value_rows, head_count, scaling, visible):
    running, summed, numerator = state_in
    query_count = queries.shape[0]
    key_count = key_rows.shape[0]
    head_size = queries.shape[1] // head_count
    scores = (
        jnp.einsum(
            "qhe,khe->hqk",
            queries.reshape(query_count, head_count, head_size),
            key_rows.reshape(key_count, head_count, head_size),
            preferred_element_type=jnp.float32,
        )
        * scaling
    )
    if visible is not None:
        scores = jnp.where(visible[None], scores, jnp.float32(-1e30))
    newest = jnp.maximum(running, jnp.max(scores, axis=2))
    shrink = jnp.exp(running - newest)
    weights = jnp.exp(scores - newest[:, :, None])
    summed = summed * shrink + jnp.sum(weights, axis=2)
    numerator = numerator * shrink[:, :, None] + jnp.einsum(
        "hqk,khe->hqe",
        weights.astype(jnp.bfloat16),
        value_rows.reshape(key_count, head_count, head_size),
        preferred_element_type=jnp.float32,
    )
    return (newest, summed, numerator)


def block_split(total_rows):
    block_rows = total_rows
    while block_rows > 512 and block_rows % 2 == 0:
        block_rows = block_rows // 2
    return (block_rows, total_rows // block_rows)


def fold_keys(state_in, shards_in, offset, queries, head_count, scaling):
    key_rows, value_rows = shards_in
    block_rows, block_count = block_split(key_rows.shape[0])
    key_blocks = key_rows.reshape(block_count, block_rows, key_rows.shape[1])
    value_blocks = value_rows.reshape(block_count, block_rows, value_rows.shape[1])

    def one_block(state, paired):
        return (absorb(state, queries, paired[0], paired[1], head_count, scaling, None), None)

    result, unused = lax.scan(one_block, state_in, (key_blocks, value_blocks))
    return result


def normalize_heads(state_in):
    running, summed, numerator = state_in
    mixed = numerator / summed[:, :, None]
    return mixed.transpose(1, 0, 2).reshape(mixed.shape[1], -1).astype(jnp.bfloat16)


def body(vid_q, vid_k, vid_v, aud_q, cross_k, cross_v, cross_q, aud_k, aud_v, windows):
    video_heads = vid_q.shape[1] // HEAD_DIM
    video_scaling = 1.0 / math.sqrt(HEAD_DIM)
    audio_heads = aud_q.shape[1] // AUDIO_DIM
    audio_scaling = 1.0 / math.sqrt(AUDIO_DIM)
    moved_q, moved_k, moved_v = (
        lax.all_to_all(vid_q, "sub", split_axis=1, concat_axis=0, tiled=True),
        lax.all_to_all(vid_k, "sub", split_axis=1, concat_axis=0, tiled=True),
        lax.all_to_all(vid_v, "sub", split_axis=1, concat_axis=0, tiled=True),
    )
    pair_heads = video_heads // lax.axis_size("sub")
    folder = partial(fold_keys, queries=moved_q, head_count=pair_heads, scaling=video_scaling)
    state = folder(
        start_state(moved_q.shape[0], pair_heads, HEAD_DIM),
        (
            lax.all_gather(moved_k, "seq", axis=0, tiled=True),
            lax.all_gather(moved_v, "seq", axis=0, tiled=True),
        ),
        jnp.int32(0),
    )
    video_self = lax.all_to_all(
        normalize_heads(state), "sub", split_axis=0, concat_axis=1, tiled=True
    )
    folder = partial(fold_keys, queries=aud_q, head_count=audio_heads, scaling=audio_scaling)
    state = folder(
        start_state(aud_q.shape[0], audio_heads, AUDIO_DIM),
        (
            lax.all_gather(cross_k, ("seq", "sub"), axis=0, tiled=True),
            lax.all_gather(cross_v, ("seq", "sub"), axis=0, tiled=True),
        ),
        jnp.int32(0),
    )
    audio_out = normalize_heads(state)
    audio_rows = aud_k.shape[0]
    key_width = aud_k.shape[1]
    padded_rows = extended(
        jnp.concatenate((aud_k, aud_v), axis=1), ((("seq", "sub"), 0),), audio_rows
    )
    near_keys = padded_rows[:, :key_width]
    near_values = padded_rows[:, key_width:]
    position = lax.axis_index(("seq", "sub"))
    audio_index = (position - 1) * audio_rows + jnp.arange(padded_rows.shape[0], dtype=jnp.int32)
    stretch_index = audio_index // STRETCH_LEN
    stretch_ids = jnp.arange(windows.shape[1], dtype=jnp.int32)
    onehot = stretch_index[:, None] == stretch_ids[None, :]
    first_tile = jnp.sum(jnp.where(onehot, windows[0][None, :], 0), axis=1)
    after_tile = jnp.sum(jnp.where(onehot, windows[1][None, :], 0), axis=1)
    video_rows = cross_q.shape[0]
    video_tile = (position * video_rows + jnp.arange(video_rows, dtype=jnp.int32)) // TILE_LEN
    visible = (first_tile[None, :] <= video_tile[:, None]) & (
        video_tile[:, None] < after_tile[None, :]
    )
    state = absorb(
        start_state(video_rows, audio_heads, AUDIO_DIM),
        cross_q,
        near_keys,
        near_values,
        audio_heads,
        audio_scaling,
        visible,
    )
    video_cross = normalize_heads(state)
    return (video_self, audio_out, video_cross)


def solution(mesh):
    return jax.shard_map(
        body,
        mesh=mesh,
        in_specs=(
            P(("grp", "seq", "sub"), "head"),
            P(("grp", "seq", "sub"), "head"),
            P(("grp", "seq", "sub"), "head"),
            P(("grp", "seq", "sub"), "head"),
            P(("grp", "seq", "sub"), "head"),
            P(("grp", "seq", "sub"), "head"),
            P(("grp", "seq", "sub"), "head"),
            P(("grp", "seq", "sub"), "head"),
            P(("grp", "seq", "sub"), "head"),
            P(None, "grp"),
        ),
        out_specs=(
            P(("grp", "seq", "sub"), "head"),
            P(("grp", "seq", "sub"), "head"),
            P(("grp", "seq", "sub"), "head"),
        ),
        check_vma=False,
    )
```

profile of v0, /device:TPU:0, one launch (start us, length us, event | category | flops | bytes accessed | tf_op | source)
XLA Modules:
  0.0 218.2 jit_solution(4391640885050590359)
XLA Ops:
  7.2 1.1 copy.138
  8.4 5.1 %all_to_all.73 = bf16[160,2,1024]{2,0,1:T(8,128)(2,1)} all-to-all(bf16[160,2,1024]{2,0,1:T(8,128)(2,1)S(1)} %bitcast.132), channel_id=1, replica_groups=mesh['grp'=2,'seq'=4,'head'=2,'sub'=2] {'sub'}, dimensions={1} | all-to-all | bytes 1310720 | tf_op jit(solution)/shard_map/all_to_all | solution.py:101
  13.7 5.1 %all_to_all.74 = bf16[160,2,1024]{2,0,1:T(8,128)(2,1)} all-to-all(bf16[160,2,1024]{2,0,1:T(8,128)(2,1)S(1)} %bitcast.133), channel_id=1, replica_groups=mesh['grp'=2,'seq'=4,'head'=2,'sub'=2] {'sub'}, dimensions={1} | all-to-all | bytes 1310720 | tf_op jit(solution)/shard_map/all_to_all | solution.py:102
  18.9 0.7 all-gather.9.cloned.1.call-update
  19.6 1.3 collective-permute-start.1
  20.9 3.7 %collective-permute-start = (bf16[40,2048]{1,0:T(8,128)(2,1)S(1)}, bf16[40,2048]{1,0:T(8,128)(2,1)}, u32[]{:S(2)}, u32[]{:S(2)}) collective-permute-start(bf16[40,2048]{1,0:T(8,128)(2,1)S(1)} %constant_dynamic-update-slice_fusion), channel_id=1, source_target_pairs={{0,1},{1,4},{4,5},{5,8},{8,9},{9,12},{12,13},{2,3},{3,6},{6,7},{7,... | collective-permute-start | bytes 491528 | tf_op jit(solution)/shard_map/ppermute | solution.py:23
  24.6 0.9 copy.137
  25.5 3.6 %all-to-all-start.1 = ((bf16[160,2,1024]{2,0,1:T(8,128)(2,1)}), bf16[160,2,1024]{2,0,1:T(8,128)(2,1)S(1)}, u32[]{:S(2)}, u32[]{:S(2)}) async-start(bf16[160,2,1024]{2,0,1:T(8,128)(2,1)} %bitcast.94), calls=%async_computation.1 | async-start | bytes 1310720 | tf_op jit(solution)/shard_map/all_to_all | solution.py:100
  29.2 0.5 all-gather.11.cloned.1.call-update
  30.3 1.0 pad_maximum_fusion
  31.4 0.8 copy.104
  32.4 0.9 fusion.37
  33.3 1.0 fusion.29
  34.3 0.6 fusion.28
  35.0 0.9 copy.105
  35.9 36.1 %all-gather.5.cloned.1.call-done = bf16[1280,1024]{1,0:T(8,128)(2,1)} async-done(((bf16[320,1024]{1,0:T(8,128)(2,1)}), bf16[1280,1024]{1,0:T(8,128)(2,1)}) %all-gather.5.cloned.1.call-update) | async-done | bytes 2621456 | tf_op jit(solution)/shard_map/all_gather | solution.py:109
  72.0 55.8 %all-gather.7.cloned.1.call-done = bf16[1280,1024]{1,0:T(8,128)(2,1)} async-done(((bf16[320,1024]{1,0:T(8,128)(2,1)}), bf16[1280,1024]{1,0:T(8,128)(2,1)}) %all-gather.7.cloned.1.call-update) | async-done | bytes 2621456 | tf_op jit(solution)/shard_map/all_gather | solution.py:110
  127.8 35.4 %while.30 = (s32[]{:T(128)}, f32[8,320]{1,0:T(8,128)S(1)}, f32[8,320]{1,0:T(8,128)S(1)}, f32[8,320,128]{2,1,0:T(8,128)S(1)}, bf16[4,320,1024]{2,1,0:T(8,128)(2,1...) while((s32[]{:T(128)}, f32[8,320]{1,0:T(8,128)S(1)}, ...), condition=%wide.region_3.4_spmd.clone, body=%wide.region_0.3_spmd.clone.sunk | while | flops 426979840 | bytes 32931984 | solution.py:84
  127.8 1.4 dynamic-slice_bitcast_fusion.3
  129.3 2.5 %bitcast_reduce_fusion.2 = (f32[8,320]{1,0:T(8,128)S(1)}, f32[8,320,320]{2,1,0:T(8,128)}) fusion(bf16[320,8,128]{2,1,0:T(8,128)(2,1)S(1)} %bitcast.123, bf16[320,1024]{1,0:T(8,128)(2,1)S(1)} %get-tuple-element.365), kind=kOutput, calls=%fused_computation.1.clone.1 | convolution fusion | flops 211351040 | bytes 4597760 | tf_op jit(solution)/shard_map/while/body/eval_jaxpr/qhe,khe->hqk/dot_general | solution.py:45
  131.8 3.0 %fusion.59 = f32[8,320]{1,0:T(8,128)S(1)} fusion(f32[8,320,320]{2,1,0:T(8,128)} %get-tuple-element.325, f32[8,320]{1,0:T(8,128)S(1)} %select_maximum_fusion.4), kind=kLoop, calls=%fused_computation.4.clone.1 | loop fusion | flops 2455040 | bytes 3297280 | tf_op jit(solution)/shard_map/while/body/eval_jaxpr/reduce_sum | solution.py:58
  135.2 1.4 fusion.61
  136.6 1.4 dynamic-slice_bitcast_fusion.3
  138.1 2.5 %bitcast_reduce_fusion.2 = (f32[8,320]{1,0:T(8,128)S(1)}, f32[8,320,320]{2,1,0:T(8,128)}) fusion(bf16[320,8,128]{2,1,0:T(8,128)(2,1)S(1)} %bitcast.123, bf16[320,1024]{1,0:T(8,128)(2,1)S(1)} %get-tuple-element.365), kind=kOutput, calls=%fused_computation.1.clone.1 | convolution fusion | flops 211351040 | bytes 4597760 | tf_op jit(solution)/shard_map/while/body/eval_jaxpr/qhe,khe->hqk/dot_general | solution.py:45
  140.7 3.0 %fusion.59 = f32[8,320]{1,0:T(8,128)S(1)} fusion(f32[8,320,320]{2,1,0:T(8,128)} %get-tuple-element.325, f32[8,320]{1,0:T(8,128)S(1)} %select_maximum_fusion.4), kind=kLoop, calls=%fused_computation.4.clone.1 | loop fusion | flops 2455040 | bytes 3297280 | tf_op jit(solution)/shard_map/while/body/eval_jaxpr/reduce_sum | solution.py:58
  144.0 1.4 fusion.61
  145.5 1.4 dynamic-slice_bitcast_fusion.3
  147.0 2.5 %bitcast_reduce_fusion.2 = (f32[8,320]{1,0:T(8,128)S(1)}, f32[8,320,320]{2,1,0:T(8,128)}) fusion(bf16[320,8,128]{2,1,0:T(8,128)(2,1)S(1)} %bitcast.123, bf16[320,1024]{1,0:T(8,128)(2,1)S(1)} %get-tuple-element.365), kind=kOutput, calls=%fused_computation.1.clone.1 | convolution fusion | flops 211351040 | bytes 4597760 | tf_op jit(solution)/shard_map/while/body/eval_jaxpr/qhe,khe->hqk/dot_general | solution.py:45
  149.5 3.0 %fusion.59 = f32[8,320]{1,0:T(8,128)S(1)} fusion(f32[8,320,320]{2,1,0:T(8,128)} %get-tuple-element.325, f32[8,320]{1,0:T(8,128)S(1)} %select_maximum_fusion.4), kind=kLoop, calls=%fused_computation.4.clone.1 | loop fusion | flops 2455040 | bytes 3297280 | tf_op jit(solution)/shard_map/while/body/eval_jaxpr/reduce_sum | solution.py:58
  152.9 1.4 fusion.61
  154.3 1.4 dynamic-slice_bitcast_fusion.3
  155.9 2.5 %bitcast_reduce_fusion.2 = (f32[8,320]{1,0:T(8,128)S(1)}, f32[8,320,320]{2,1,0:T(8,128)}) fusion(bf16[320,8,128]{2,1,0:T(8,128)(2,1)S(1)} %bitcast.123, bf16[320,1024]{1,0:T(8,128)(2,1)S(1)} %get-tuple-element.365), kind=kOutput, calls=%fused_computation.1.clone.1 | convolution fusion | flops 211351040 | bytes 4597760 | tf_op jit(solution)/shard_map/while/body/eval_jaxpr/qhe,khe->hqk/dot_general | solution.py:45
  158.4 3.0 %fusion.59 = f32[8,320]{1,0:T(8,128)S(1)} fusion(f32[8,320,320]{2,1,0:T(8,128)} %get-tuple-element.325, f32[8,320]{1,0:T(8,128)S(1)} %select_maximum_fusion.4), kind=kLoop, calls=%fused_computation.4.clone.1 | loop fusion | flops 2455040 | bytes 3297280 | tf_op jit(solution)/shard_map/while/body/eval_jaxpr/reduce_sum | solution.py:58
  161.7 1.4 fusion.61
  163.2 0.4 fusion.33
  163.6 0.4 copy.97
  164.3 4.4 %all_to_all.75 = bf16[2,160,1024]{2,1,0:T(8,128)(2,1)S(1)} all-to-all(bf16[2,160,1024]{2,1,0:T(8,128)(2,1)S(1)} %convert_element_type.36), channel_id=1, replica_groups=mesh['grp'=2,'seq'=4,'head'=2,'sub'=2] {'sub'}, dimensions={0} | all-to-all | bytes 1310720 | tf_op jit(solution)/shard_map/all_to_all | solution.py:114
  168.7 0.9 copy.116
  169.6 26.7 %all-gather.11.cloned.1.call-done = bf16[1280,1024]{1,0:T(8,128)(2,1)} async-done(((bf16[160,1024]{1,0:T(8,128)(2,1)}), bf16[1280,1024]{1,0:T(8,128)(2,1)}) %all-gather.11.cloned.1.call-update) | async-done | bytes 2621456 | tf_op jit(solution)/shard_map/all_gather | solution.py:122
  196.3 14.4 %while.31 = (s32[]{:T(128)}, f32[16,40]{1,0:T(8,128)S(1)}, f32[16,40]{1,0:T(8,128)S(1)}, f32[16,40,64]{2,1,0:T(8,128)S(1)}, bf16[4,320,1024]{2,1,0:T(8,128)(2,1)...) while((s32[]{:T(128)}, f32[16,40]{1,0:T(8,128)S(1)}, ...), condition=%wide.region_7.8_spmd.clone, body=%wide.region_4.7_spmd.clone.sunk | while | flops 53783680 | bytes 9625717 | solution.py:84
  196.3 1.4 constant_dynamic-slice_fusion.3
  197.7 0.4 copy.153
  198.2 0.4 fusion.65
  198.6 0.4 fusion.66
  199.0 0.4 copy.154
  199.4 0.5 convolution_add_fusion.2
  199.9 1.4 constant_dynamic-slice_fusion.3
  201.3 0.4 copy.153
  201.8 0.4 fusion.65
  202.2 0.4 fusion.66
  203.0 0.5 convolution_add_fusion.2
  203.5 1.4 constant_dynamic-slice_fusion.3
  204.9 0.4 copy.153
  205.4 0.4 fusion.65
  205.8 0.4 fusion.66
  206.2 0.4 copy.154
  206.6 0.5 convolution_add_fusion.2
  207.1 1.4 constant_dynamic-slice_fusion.3
  208.5 0.4 copy.153
  209.0 0.4 fusion.65
  209.4 0.4 fusion.66
  209.8 0.4 copy.154
  210.2 0.5 convolution_add_fusion.2
  210.9 0.8 convert_element_type.39
  (93 shorter events, 4.4 us)
Async XLA Ops:
  7.2 64.8 %all-gather.5.cloned.1.call-start = ((), (), s32[]{:S(2)}) async-start(), calls=%async_computation.4 | async-start | bytes 3276800 | tf_op jit(solution)/shard_map/all_gather | solution.py:109
  8.3 5.2 %copy-start.2 = (bf16[160,2048]{1,0:T(8,128)(2,1)S(1)}, bf16[160,2048]{1,0:T(8,128)(2,1)}, u32[]{:S(2)}) copy-start(bf16[160,2048]{1,0:T(8,128)(2,1)} %param.16) | copy-start | bytes 1966084
  13.5 114.2 %all-gather.7.cloned.1.call-start = ((), (), s32[]{:S(2)}) async-start(), calls=%async_computation.5 | async-start | bytes 3276800 | tf_op jit(solution)/shard_map/all_gather | solution.py:110
  13.6 5.9 %copy-start.6 = (bf16[40,1024]{1,0:T(8,128)(2,1)S(1)}, bf16[40,1024]{1,0:T(8,128)(2,1)}, u32[]{:S(2)}) copy-start(bf16[40,1024]{1,0:T(8,128)(2,1)} %param.21) | copy-start | bytes 245764
  13.7 6.0 %copy-start.7 = (bf16[40,1024]{1,0:T(8,128)(2,1)S(1)}, bf16[40,1024]{1,0:T(8,128)(2,1)}, u32[]{:S(2)}) copy-start(bf16[40,1024]{1,0:T(8,128)(2,1)} %param.22) | copy-start | bytes 245764
  13.7 11.0 %copy-start.3 = (bf16[160,2048]{1,0:T(8,128)(2,1)S(1)}, bf16[160,2048]{1,0:T(8,128)(2,1)}, u32[]{:S(2)}) copy-start(bf16[160,2048]{1,0:T(8,128)(2,1)} %param.14) | copy-start | bytes 1966084
  18.8 150.8 %all-gather.9.cloned.1.call-start = ((), (), s32[]{:S(2)}) async-start(), calls=%async_computation.6 | async-start | bytes 2949120 | tf_op jit(solution)/shard_map/all_gather | solution.py:121
  19.6 10.7 %collective-permute-start.1 = (bf16[40,2048]{1,0:T(8,128)(2,1)S(1)}, bf16[40,2048]{1,0:T(8,128)(2,1)}, u32[]{:S(2)}, u32[]{:S(2)}) collective-permute-start(bf16[40,2048]{1,0:T(8,128)(2,1)S(1)} %constant_dynamic-update-slice_fusion), channel_id=1, source_target_pairs={{1,0},{4,1},{5,4},{8,5},{9,8},{12,9},{13,12},{3,2},{6,3},{7,6},{10... | collective-permute-start | bytes 491528 | tf_op jit(solution)/shard_map/ppermute | solution.py:25
  20.9 9.4 %collective-permute-start = (bf16[40,2048]{1,0:T(8,128)(2,1)S(1)}, bf16[40,2048]{1,0:T(8,128)(2,1)}, u32[]{:S(2)}, u32[]{:S(2)}) collective-permute-start(bf16[40,2048]{1,0:T(8,128)(2,1)S(1)} %constant_dynamic-update-slice_fusion), channel_id=1, source_target_pairs={{0,1},{1,4},{4,5},{5,8},{8,9},{9,12},{12,13},{2,3},{3,6},{6,7},{7,... | collective-permute-start | bytes 491528 | tf_op jit(solution)/shard_map/ppermute | solution.py:23
  24.6 5.2 %copy-start.4 = (bf16[160,1024]{1,0:T(8,128)(2,1)S(1)}, bf16[160,1024]{1,0:T(8,128)(2,1)}, u32[]{:S(2)}) copy-start(bf16[160,1024]{1,0:T(8,128)(2,1)} %param.20) | copy-start | bytes 983044
  25.5 4.5 %copy-start.8 = (s32[2,40]{1,0:T(2,128)S(1)}, s32[2,40]{1,0:T(2,128)}, u32[]{:S(2)}) copy-start(s32[2,40]{1,0:T(2,128)} %param.23) | copy-start | bytes 964
  25.5 10.4 %all-to-all-start.1 = ((bf16[160,2,1024]{2,0,1:T(8,128)(2,1)}), bf16[160,2,1024]{2,0,1:T(8,128)(2,1)S(1)}, u32[]{:S(2)}, u32[]{:S(2)}) async-start(bf16[160,2,1024]{2,0,1:T(8,128)(2,1)} %bitcast.94), calls=%async_computation.1 | async-start | bytes 1310720 | tf_op jit(solution)/shard_map/all_to_all | solution.py:100
  29.2 167.1 %all-gather.11.cloned.1.call-start = ((), (), s32[]{:S(2)}) async-start(), calls=%async_computation.7 | async-start | bytes 2949120 | tf_op jit(solution)/shard_map/all_gather | solution.py:122
  32.4 1.9 copy-start.5
  131.8 3.4 %copy-start = (f32[8,320,320]{2,1,0:T(8,128)S(1)}, f32[8,320,320]{2,1,0:T(8,128)}, u32[]{:S(2)}) copy-start(f32[8,320,320]{2,1,0:T(8,128)} %get-tuple-element.325) | copy-start | bytes 9830404 | tf_op jit(solution)/shard_map/while
  140.7 3.4 %copy-start = (f32[8,320,320]{2,1,0:T(8,128)S(1)}, f32[8,320,320]{2,1,0:T(8,128)}, u32[]{:S(2)}) copy-start(f32[8,320,320]{2,1,0:T(8,128)} %get-tuple-element.325) | copy-start | bytes 9830404 | tf_op jit(solution)/shard_map/while
  149.5 3.4 %copy-start = (f32[8,320,320]{2,1,0:T(8,128)S(1)}, f32[8,320,320]{2,1,0:T(8,128)}, u32[]{:S(2)}) copy-start(f32[8,320,320]{2,1,0:T(8,128)} %get-tuple-element.325) | copy-start | bytes 9830404 | tf_op jit(solution)/shard_map/while
  158.4 3.3 %copy-start = (f32[8,320,320]{2,1,0:T(8,128)S(1)}, f32[8,320,320]{2,1,0:T(8,128)}, u32[]{:S(2)}) copy-start(f32[8,320,320]{2,1,0:T(8,128)} %get-tuple-element.325) | copy-start | bytes 9830404 | tf_op jit(solution)/shard_map/while
  164.3 32.0 %copy-start.1 = (bf16[40,1024]{1,0:T(8,128)(2,1)S(1)}, bf16[40,1024]{1,0:T(8,128)(2,1)}, u32[]{:S(2)}) copy-start(bf16[40,1024]{1,0:T(8,128)(2,1)} %param.17) | copy-start | bytes 245764
Sparse Core Ops, SparseCore 0:
  13.6 58.2 all-gather.4
  73.6 54.1 all-gather.6
  129.4 32.4 all-gather.8
  163.4 32.8 all-gather.10
where the time goes:
time: 219 us; the launch traced here: 218 us
  waiting for transfers between devices  120 us (55%)
  local copies, waits for them, and re-layouts  23.1 us (11%)
  matrix products  20.8 us (9%)
  other arithmetic  16.4 us (7%)
  blocking collectives  14.7 us (7%)
  between operations  14.1 us (6%)
  starting transfers between devices  8.81 us (4%)
    all_gather x1, waiting for transfers between devices, body(): lax.all_gather(moved_v, 'seq', axis=0, tiled=True)  55.8 us
    all_gather x1, waiting for transfers between devices, body(): lax.all_gather(moved_k, 'seq', axis=0, tiled=True)  36.1 us
    all_gather x1, waiting for transfers between devices, body(): lax.all_gather(cross_v, ('seq', 'sub'), axis=0, tiled=True)  26.7 us
    reduce_sum x9, other arithmetic, absorb(): summed = summed * shrink + jnp.sum(weights, axis=2)  14.4 us
    dot_general x9, matrix products, absorb(): jnp.einsum('qhe,khe->hqk', queries.reshape(query_count, head_count, head_...  12.6 us
    dynamic_slice x12, local copies, waits for them, and re-layouts, fold_keys(): result, unused = lax.scan(one_block, state_in, (key_blocks, value_blocks))  8.35 us
    dot_general x9, matrix products, absorb(): jnp.einsum('hqk,khe->hqe', weights.astype(jnp.bfloat16), value_rows.resha...  8.23 us
    while x28, local copies, waits for them, and re-layouts  7.43 us
  transfers between devices with their start and end apart: 7, of which 3 were waited for; matrix products, arithmetic and copies ran while one was open for 20% of the time, Pallas kernels for 0%

commit v1 on v0

--- a/solution.py
+++ b/solution.py
@@ -4,6 +4,8 @@
 import jax
 import jax.numpy as jnp
 from jax import lax
+from jax.experimental import pallas as pl
+from jax.experimental.pallas import tpu as pltpu
 from jax.sharding import PartitionSpec as P
 
 HEAD_DIM = 128
@@ -91,7 +93,7 @@
     return mixed.transpose(1, 0, 2).reshape(mixed.shape[1], -1).astype(jnp.bfloat16)
 
 
-def body(vid_q, vid_k, vid_v, aud_q, cross_k, cross_v, cross_q, aud_k, aud_v, windows):
+def gathered_body(vid_q, vid_k, vid_v, aud_q, cross_k, cross_v, cross_q, aud_k, aud_v, windows):
     video_heads = vid_q.shape[1] // HEAD_DIM
     video_scaling = 1.0 / math.sqrt(HEAD_DIM)
     audio_heads = aud_q.shape[1] // AUDIO_DIM
@@ -156,6 +158,396 @@
     return (video_self, audio_out, video_cross)
 
 
+LANES = 128
+AXES = ("seq", "sub")
+
+
+def softmax_mix(queries, key_rows, value_rows, scaling, visible=None):
+    scores = lax.dot_general(
+        queries, key_rows, (((1,), (1,)), ((), ())), preferred_element_type=jnp.float32
+    )
+    if visible is not None:
+        scores = jnp.where(visible, scores, jnp.float32(-1e30))
+    peak = jnp.max(scores, axis=1, keepdims=True)
+    weights = jnp.exp2((scores - peak) * jnp.float32(scaling * math.log2(math.e)))
+    summed = jnp.sum(weights, axis=1, keepdims=True)
+    mixed = jnp.dot(
+        weights.astype(jnp.bfloat16), value_rows, preferred_element_type=jnp.float32
+    )
+    return mixed / summed
+
+
+def lane_heads(block):
+    wide = block.astype(jnp.float32)
+    lane = lax.broadcasted_iota(jnp.int32, wide.shape, 1) // AUDIO_DIM
+    parts = [jnp.where(lane == i, wide, 0.0) for i in range(LANES // AUDIO_DIM)]
+    return jnp.concatenate(parts, axis=0).astype(jnp.bfloat16)
+
+
+def merge_lane_heads(stacked, rows):
+    lane = lax.broadcasted_iota(jnp.int32, (rows, LANES), 1) // AUDIO_DIM
+    merged = stacked[:rows]
+    for i in range(1, LANES // AUDIO_DIM):
+        merged = jnp.where(lane == i, stacked[i * rows : (i + 1) * rows], merged)
+    return merged
+
+
+def exchange_kernel(
+    count,
+    sub_count,
+    vid_q,
+    vid_k,
+    vid_v,
+    aud_q,
+    cross_k,
+    cross_v,
+    cross_q,
+    aud_k,
+    aud_v,
+    windows,
+    video_self,
+    audio_out,
+    video_cross,
+    land_q,
+    land_k,
+    land_v,
+    land_aq,
+    land_ck,
+    land_cv,
+    mixed_v,
+    mixed_a,
+    near_k,
+    near_v,
+    local_cq,
+    mixed_c,
+    send_sem,
+    recv_sem,
+    near_send,
+    near_recv,
+    local_sem,
+):
+    rows = vid_q.shape[0]
+    audio_rows = aud_q.shape[0]
+    video_each = vid_q.shape[1] // HEAD_DIM // count
+    blocks_each = aud_q.shape[1] // LANES // count
+    video_scaling = 1.0 / math.sqrt(HEAD_DIM)
+    audio_scaling = 1.0 / math.sqrt(AUDIO_DIM)
+    me = lax.axis_index("seq") * sub_count + lax.axis_index("sub")
+
+    def device(peer):
+        return {"seq": peer // sub_count, "sub": peer % sub_count}
+
+    def peer_at(t):
+        half = (t + 1) // 2
+        return (me + count // 2 + (1 - 2 * (t % 2)) * half) % count
+
+    barrier = pltpu.get_barrier_semaphore()
+
+    def greet(t, carry):
+        pl.semaphore_signal(
+            barrier, inc=1, device_id=device(peer_at(t)), device_id_type=pl.DeviceIdType.MESH
+        )
+        return carry
+
+    lax.fori_loop(0, count - 1, greet, 0)
+
+    own = [
+        pltpu.make_async_copy(cross_q, local_cq, local_sem.at[0]),
+        pltpu.make_async_copy(aud_k, near_k.at[1], local_sem.at[1]),
+        pltpu.make_async_copy(aud_v, near_v.at[1], local_sem.at[2]),
+    ]
+    for copy in own:
+        copy.start()
+
+    def column(index):
+        return pl.ds(pl.multiple_of(index * LANES, LANES), LANES)
+
+    def row(index):
+        return pl.ds(pl.multiple_of(index * rows, rows), rows)
+
+    streams = []
+    for h in range(video_each):
+        for array, land in ((vid_k, land_k), (vid_v, land_v), (vid_q, land_q)):
+            streams.append(
+                (
+                    lambda peer, array=array, h=h: array.at[:, column(peer * video_each + h)],
+                    lambda source, land=land, h=h: land.at[h, row(source), :],
+                )
+            )
+    for b in range(blocks_each):
+        for array, land in ((cross_k, land_ck), (cross_v, land_cv)):
+            streams.append(
+                (
+                    lambda peer, array=array, b=b: array.at[:, column(peer * blocks_each + b)],
+                    lambda source, land=land, b=b: land.at[b, row(source), :],
+                )
+            )
+        streams.append(
+            (
+                lambda peer, b=b: aud_q.at[:, column(peer * blocks_each + b)],
+                lambda source, b=b: land_aq.at[b, source],
+            )
+        )
+    results = []
+    for h in range(video_each):
+        results.append(
+            (
+                lambda peer, h=h: mixed_v.at[h, row(peer), :],
+                lambda source, h=h: video_self.at[:, column(source * video_each + h)],
+            )
+        )
+    for b in range(blocks_each):
+        results.append(
+            (
+                lambda peer, b=b: mixed_a.at[b, peer],
+                lambda source, b=b: audio_out.at[:, column(source * blocks_each + b)],
+            )
+        )
+    ways = streams + results
+
+    def outgoing(k, peer):
+        return pltpu.make_async_remote_copy(
+            src_ref=ways[k][0](peer),
+            dst_ref=ways[k][1](me),
+            send_sem=send_sem.at[k, peer],
+            recv_sem=recv_sem.at[k, me],
+            device_id=device(peer),
+            device_id_type=pl.DeviceIdType.MESH,
+        )
+
+    def incoming(k, peer):
+        return pltpu.make_async_remote_copy(
+            src_ref=ways[k][0](peer),
+            dst_ref=ways[k][1](peer),
+            send_sem=send_sem.at[k, peer],
+            recv_sem=recv_sem.at[k, peer],
+            device_id=device(peer),
+            device_id_type=pl.DeviceIdType.MESH,
+        )
+
+    def kept(k):
+        return pltpu.make_async_copy(ways[k][0](me), ways[k][1](me), send_sem.at[k, me])
+
+    def near_copy(j, array, near, side, peer):
+        return pltpu.make_async_remote_copy(
+            src_ref=array,
+            dst_ref=near.at[side],
+            send_sem=near_send.at[j],
+            recv_sem=near_recv.at[j],
+            device_id=device(peer),
+            device_id_type=pl.DeviceIdType.MESH,
+        )
+
+    for k in range(len(streams)):
+        kept(k).start()
+    pl.semaphore_wait(barrier, count - 1)
+
+    near_pairs = ((0, aud_k, near_k), (1, aud_v, near_v))
+
+    @pl.when(me < count - 1)
+    def _():
+        for j, array, near in near_pairs:
+            near_copy(j, array, near, 0, me + 1).start()
+
+    @pl.when(me > 0)
+    def _():
+        for j, array, near in near_pairs:
+            near_copy(2 + j, array, near, 2, me - 1).start()
+
+    for k in range(len(streams)):
+
+        def send(t, carry, k=k):
+            outgoing(k, peer_at(t)).start()
+            return carry
+
+        lax.fori_loop(0, count - 1, send, 0)
+
+    @pl.when(me == 0)
+    def _():
+        for j, array, near in near_pairs:
+            near[0] = jnp.zeros(near.shape[1:], near.dtype)
+
+    @pl.when(me == count - 1)
+    def _():
+        for j, array, near in near_pairs:
+            near[2] = jnp.zeros(near.shape[1:], near.dtype)
+
+    for copy in own:
+        copy.wait()
+
+    @pl.when(me > 0)
+    def _():
+        for j, array, near in near_pairs:
+            near_copy(j, array, near, 0, me - 1).wait_recv()
+
+    @pl.when(me < count - 1)
+    def _():
+        for j, array, near in near_pairs:
+            near_copy(2 + j, array, near, 2, me + 1).wait_recv()
+
+    spans = windows.shape[1]
+    tile = (me * rows + lax.broadcasted_iota(jnp.int32, (rows, spans), 0)) // TILE_LEN
+    bounds = windows[...]
+    inside = (bounds[0:1, :] <= tile) & (tile < bounds[1:2, :])
+    inside = jnp.where(inside, 1.0, 0.0).astype(jnp.bfloat16)
+    seen = []
+    for side in range(3):
+        stretch = lax.broadcasted_iota(jnp.int32, (spans, audio_rows), 1) // STRETCH_LEN
+        stretch = stretch + (me + side - 1) * (audio_rows // STRETCH_LEN)
+        picks = stretch == lax.broadcasted_iota(jnp.int32, (spans, audio_rows), 0)
+        picks = jnp.where(picks, 1.0, 0.0).astype(jnp.bfloat16)
+        part = jnp.dot(inside, picks, preferred_element_type=jnp.float32)
+        seen.append(jnp.concatenate([part] * (LANES // AUDIO_DIM), axis=0))
+
+    for b in range(cross_q.shape[1] // LANES):
+        lanes = slice(b * LANES, (b + 1) * LANES)
+        stacked = lane_heads(local_cq[:, lanes])
+        scores = []
+        for side in range(3):
+            part = lax.dot_general(
+                stacked,
+                near_k[side, :, lanes],
+                (((1,), (1,)), ((), ())),
+                preferred_element_type=jnp.float32,
+            )
+            scores.append(jnp.where(seen[side] > 0.5, part, jnp.float32(-1e30)))
+        peak = jnp.max(jnp.maximum(jnp.maximum(scores[0], scores[1]), scores[2]), axis=1, keepdims=True)
+        factor = jnp.float32(audio_scaling * math.log2(math.e))
+        weights = [jnp.exp2((part - peak) * factor) for part in scores]
+        summed = jnp.sum(weights[0] + weights[1] + weights[2], axis=1, keepdims=True)
+        mixed = sum(
+            jnp.dot(
+                weights[side].astype(jnp.bfloat16),
+                near_v[side, :, lanes],
+                preferred_element_type=jnp.float32,
+            )
+            for side in range(3)
+        )
+        mixed_c[:, lanes] = merge_lane_heads(mixed / summed, rows).astype(jnp.bfloat16)
+
+    def await_stream(k):
+        kept(k).wait()
+
+        def one(t, carry):
+            incoming(k, peer_at(t)).wait_recv()
+            return carry
+
+        lax.fori_loop(0, count - 1, one, 0)
+
+    def run_blocks(k, mix):
+        def one(t, carry):
+            mix(peer_at(t))
+
+            @pl.when(t > 0)
+            def _():
+                outgoing(k, peer_at(t - 1)).start()
+
+            return carry
+
+        lax.fori_loop(0, count, one, 0)
+
+    first = len(streams)
+    for h in range(video_each):
+        for k in range(3 * h, 3 * h + 3):
+            await_stream(k)
+
+        def mix_video(source, h=h):
+            mixed = softmax_mix(land_q[h, row(source), :], land_k[h], land_v[h], video_scaling)
+            mixed_v[h, row(source), :] = mixed.astype(jnp.bfloat16)
+
+        run_blocks(first + h, mix_video)
+        if h == 0:
+            finished = pltpu.make_async_copy(mixed_c, video_cross, local_sem.at[0])
+            finished.start()
+    for b in range(blocks_each):
+        base = 3 * video_each + 3 * b
+        for k in range(base, base + 3):
+            await_stream(k)
+
+        def mix_audio(source, b=b):
+            mixed = softmax_mix(
+                lane_heads(land_aq[b, source]), land_ck[b], land_cv[b], audio_scaling
+            )
+            mixed_a[b, source] = merge_lane_heads(mixed, audio_rows).astype(jnp.bfloat16)
+
+        run_blocks(first + video_each + b, mix_audio)
+    for k in range(first, len(ways)):
+        kept(k).start()
+
+    for k in range(len(ways)):
+
+        def sent(t, carry, k=k):
+            outgoing(k, peer_at(t)).wait_send()
+            return carry
+
+        lax.fori_loop(0, count - 1, sent, 0)
+    for k in range(first, len(ways)):
+        await_stream(k)
+    finished.wait()
+
+    @pl.when(me < count - 1)
+    def _():
+        for j, array, near in near_pairs:
+            near_copy(j, array, near, 0, me + 1).wait_send()
+
+    @pl.when(me > 0)
+    def _():
+        for j, array, near in near_pairs:
+            near_copy(2 + j, array, near, 2, me - 1).wait_send()
+
+
+def exchanged_body(count, sub_count, *arrays):
+    vid_q, vid_k, vid_v, aud_q, cross_k, cross_v, cross_q, aud_k, aud_v, windows = arrays
+    rows = vid_q.shape[0]
+    audio_rows = aud_q.shape[0]
+    video_each = vid_q.shape[1] // HEAD_DIM // count
+    blocks_each = aud_q.shape[1] // LANES // count
+    kinds = 4 * video_each + 4 * blocks_each
+    half = jnp.bfloat16
+    place = pl.BlockSpec(memory_space=pl.ANY)
+    return pl.pallas_call(
+        partial(exchange_kernel, count, sub_count),
+        out_shape=(
+            jax.ShapeDtypeStruct(vid_q.shape, half),
+            jax.ShapeDtypeStruct(aud_q.shape, half),
+            jax.ShapeDtypeStruct(cross_q.shape, half),
+        ),
+        in_specs=[place] * 9 + [pl.BlockSpec(memory_space=pltpu.VMEM)],
+        out_specs=(place, place, place),
+        scratch_shapes=[
+            pltpu.VMEM((video_each, count * rows, HEAD_DIM), half),
+            pltpu.VMEM((video_each, count * rows, HEAD_DIM), half),
+            pltpu.VMEM((video_each, count * rows, HEAD_DIM), half),
+            pltpu.VMEM((blocks_each, count, audio_rows, LANES), half),
+            pltpu.VMEM((blocks_each, count * rows, LANES), half),
+            pltpu.VMEM((blocks_each, count * rows, LANES), half),
+            pltpu.VMEM((video_each, count * rows, HEAD_DIM), half),
+            pltpu.VMEM((blocks_each, count, audio_rows, LANES), half),
+            pltpu.VMEM((3, audio_rows, aud_k.shape[1]), half),
+            pltpu.VMEM((3, audio_rows, aud_k.shape[1]), half),
+            pltpu.VMEM(cross_q.shape, half),
+            pltpu.VMEM(cross_q.shape, half),
+            pltpu.SemaphoreType.DMA((kinds, count)),
+            pltpu.SemaphoreType.DMA((kinds, count)),
+            pltpu.SemaphoreType.DMA((4,)),
+            pltpu.SemaphoreType.DMA((4,)),
+            pltpu.SemaphoreType.DMA((3,)),
+        ],
+        compiler_params=pltpu.CompilerParams(collective_id=0, has_side_effects=True),
+        name="joint_attention",
+    )(*arrays)
+
+
+def body(*arrays):
+    sub_count = lax.axis_size("sub")
+    count = lax.axis_size("seq") * sub_count
+    video_heads = arrays[0].shape[1] // HEAD_DIM
+    audio_blocks = arrays[3].shape[1] // LANES
+    if video_heads % count == 0 and audio_blocks % count == 0:
+        return exchanged_body(count, sub_count, *arrays)
+    return gathered_body(*arrays)
+
+
 def solution(mesh):
     return jax.shard_map(
         body,

time: 219 us -> 88.8 us (0.41)
  waiting for transfers between devices: 120 us -> 0 us
  Pallas kernels: 0 us -> 84.6 us
  matrix products: 20.8 us -> 0 us
  local copies, waits for them, and re-layouts: 23.1 us -> 3.4 us
  other arithmetic: 16.4 us -> 0 us
  blocking collectives: 14.7 us -> 0 us
  between operations: 14.1 us -> 0.66 us
  starting transfers between devices: 8.81 us -> 0 us
    all_gather x4 -> x0, waiting for transfers between devices: 119 us -> none  [the longest x1 55.8 us: body(): lax.all_gather(moved_v, 'seq', axis=0, tiled=True)]
    pallas_call x0 -> x1, Pallas kernels: none -> 84.6 us  [exchanged_body(): pl.pallas_call(partial(exchange_kernel, count, sub_count), out_shape=(jax...]
    dot_general x18 -> x0, matrix products: 20.8 us -> none  [the longest x9 12.6 us: absorb(): jnp.einsum('qhe,khe->hqk', queries.reshape(query_count, head_count, head_...]
    all_to_all x3 -> x0, blocking collectives: 14.7 us -> none  [the longest x1 5.14 us: body(): lax.all_to_all(vid_k, 'sub', split_axis=1, concat_axis=0, tiled=True)]
    reduce_sum x10 -> x0, other arithmetic: 14.5 us -> none  [the longest x9 14.4 us: absorb(): summed = summed * shrink + jnp.sum(weights, axis=2)]
    dynamic_slice x12 -> x0, local copies, waits for them, and re-layouts: 8.35 us -> none  [fold_keys(): result, unused = lax.scan(one_block, state_in, (key_blocks, value_blocks))]
    while x28 -> x0, local copies, waits for them, and re-layouts: 7.43 us -> none
    ppermute x2 -> x0, starting transfers between devices: 5 us -> none  [the longest x1 3.71 us: extended(): lax.ppermute(tail, axis, [(i, (i + 1) % count) for i in range(ends)])]
  transfers between devices with their start and end apart: 7 -> 0, of which waited for: 3 -> 0; matrix products, arithmetic and copies ran while one was open for 20% -> 0% of each run, Pallas kernels for 0% -> 0%
where the time goes in v1:
time: 88.8 us; the launch traced here: 88.7 us
  Pallas kernels  84.6 us (95%)
  local copies, waits for them, and re-layouts  3.4 us (4%)
    pallas_call x1, Pallas kernels, exchanged_body(): pl.pallas_call(partial(exchange_kernel, count, sub_count), out_shape=(jax...  84.6 us
    unnamed x7, local copies, waits for them, and re-layouts  3.4 us

profile of v1, /device:TPU:0, one launch (start us, length us, event | category | flops | bytes accessed | tf_op | source)
XLA Modules:
  0.0 88.7 jit_solution(17750761642490019287)
XLA Ops:
  0.6 84.6 %joint_attention.1 = (bf16[160,2048]{1,0:T(8,128)(2,1)}, bf16[40,1024]{1,0:T(8,128)(2,1)}, bf16[160,1024]{1,0:T(8,128)(2,1)}) custom-call(bf16[160,2048]{1,0:T(8,128)(2,1)} %vid_q.1, bf16[160,2048]{1,0:T(8,128)(2,1)} %vid_k.1, bf16[160,2048]{1,0:T(8,128)(2,1)} %vid_v.1, bf16[40,1024]{1,0:T(8,128)(2,1)} %aud_q.1, bf16[160,1024]{1,0:T(8,128)(2,1)} %cross_k.1, ...), custom_call_target="tpu_custom_call" | custom-call | tf_op jit(solution)/shard_map/joint_attention/pallas_call | solution.py:508
  85.3 0.0 copy-start.1
  85.3 0.0 copy-start
  85.3 2.0 %copy.16 = bf16[160,2048]{1,0:T(8,128)(2,1)} copy(bf16[160,2048]{1,0:T(8,128)(2,1)} %get-tuple-element.6) | data formatting | bytes 1310720
  87.3 0.0 copy-done.1
  87.3 0.6 copy.17
  88.0 0.0 copy-done
  88.0 0.7 copy.18
Async XLA Ops:
  85.3 2.1 %copy-start.1 = (bf16[40,1024]{1,0:T(8,128)(2,1)S(1)}, bf16[40,1024]{1,0:T(8,128)(2,1)}, u32[]{:S(2)}) copy-start(bf16[40,1024]{1,0:T(8,128)(2,1)} %get-tuple-element.7) | copy-start | bytes 245764
  85.3 2.7 %copy-start = (bf16[160,1024]{1,0:T(8,128)(2,1)S(1)}, bf16[160,1024]{1,0:T(8,128)(2,1)}, u32[]{:S(2)}) copy-start(bf16[160,1024]{1,0:T(8,128)(2,1)} %get-tuple-element.8) | copy-start | bytes 983044

commit v2 on v1

--- a/solution.py
+++ b/solution.py
@@ -162,19 +162,17 @@
 AXES = ("seq", "sub")
 
 
-def softmax_mix(queries, key_rows, value_rows, scaling, visible=None):
+def softmax_mix(queries, key_rows, value_rows, scaling):
     scores = lax.dot_general(
         queries, key_rows, (((1,), (1,)), ((), ())), preferred_element_type=jnp.float32
     )
-    if visible is not None:
-        scores = jnp.where(visible, scores, jnp.float32(-1e30))
     peak = jnp.max(scores, axis=1, keepdims=True)
     weights = jnp.exp2((scores - peak) * jnp.float32(scaling * math.log2(math.e)))
     summed = jnp.sum(weights, axis=1, keepdims=True)
     mixed = jnp.dot(
         weights.astype(jnp.bfloat16), value_rows, preferred_element_type=jnp.float32
     )
-    return mixed / summed
+    return mixed / summed, peak, summed
 
 
 def lane_heads(block):
@@ -216,6 +214,12 @@
     land_cv,
     mixed_v,
     mixed_a,
+    own_part,
+    own_stat,
+    far_part,
+    far_stat,
+    got_part,
+    got_stat,
     near_k,
     near_v,
     local_cq,
@@ -224,22 +228,31 @@
     recv_sem,
     near_send,
     near_recv,
+    part_send,
+    part_recv,
     local_sem,
 ):
     rows = vid_q.shape[0]
     audio_rows = aud_q.shape[0]
     video_each = vid_q.shape[1] // HEAD_DIM // count
-    blocks_each = aud_q.shape[1] // LANES // count
+    half = count // 2
+    blocks_each = aud_q.shape[1] // LANES // half
+    width = blocks_each * LANES
     video_scaling = 1.0 / math.sqrt(HEAD_DIM)
     audio_scaling = 1.0 / math.sqrt(AUDIO_DIM)
     me = lax.axis_index("seq") * sub_count + lax.axis_index("sub")
 
+    side = me // half
+    place = me % half
+
     def device(peer):
         return {"seq": peer // sub_count, "sub": peer % sub_count}
 
     def peer_at(t):
-        half = (t + 1) // 2
-        return (me + count // 2 + (1 - 2 * (t % 2)) * half) % count
+        return (me + half + (1 - 2 * (t % 2)) * ((t + 1) // 2)) % count
+
+    def peer_near(t):
+        return side * half + (place + 1 + t) % half
 
     barrier = pltpu.get_barrier_semaphore()
 
@@ -265,45 +278,61 @@
     def row(index):
         return pl.ds(pl.multiple_of(index * rows, rows), rows)
 
-    streams = []
+    def columns(index):
+        return pl.ds(pl.multiple_of(index * width, LANES), width)
+
+    def video_way(array, land, h):
+        return (
+            lambda peer: array.at[:, column(peer * video_each + h)],
+            lambda source: land.at[h, row(source), :],
+            peer_at,
+            count - 1,
+        )
+
+    def half_way(array, land):
+        return (
+            lambda peer: array.at[:, columns(peer % half)],
+            lambda source: land.at[row(source % half), :],
+            peer_near,
+            half - 1,
+        )
+
+    ways = [
+        (
+            lambda peer: aud_q.at[:, columns(peer % half)],
+            lambda source: land_aq.at[source],
+            peer_at,
+            count - 1,
+        )
+    ]
+    audio_ways = [0]
+    video_ways = []
     for h in range(video_each):
+        video_ways.append(list(range(len(ways), len(ways) + 3)))
         for array, land in ((vid_k, land_k), (vid_v, land_v), (vid_q, land_q)):
-            streams.append(
-                (
-                    lambda peer, array=array, h=h: array.at[:, column(peer * video_each + h)],
-                    lambda source, land=land, h=h: land.at[h, row(source), :],
-                )
-            )
-    for b in range(blocks_each):
-        for array, land in ((cross_k, land_ck), (cross_v, land_cv)):
-            streams.append(
-                (
-                    lambda peer, array=array, b=b: array.at[:, column(peer * blocks_each + b)],
-                    lambda source, land=land, b=b: land.at[b, row(source), :],
-                )
-            )
-        streams.append(
-            (
-                lambda peer, b=b: aud_q.at[:, column(peer * blocks_each + b)],
-                lambda source, b=b: land_aq.at[b, source],
-            )
-        )
-    results = []
+            ways.append(video_way(array, land, h))
+        if h == 0:
+            for array, land in ((cross_k, land_ck), (cross_v, land_cv)):
+                audio_ways.append(len(ways))
+                ways.append(half_way(array, land))
+    first = len(ways)
     for h in range(video_each):
-        results.append(
+        ways.append(
             (
                 lambda peer, h=h: mixed_v.at[h, row(peer), :],
                 lambda source, h=h: video_self.at[:, column(source * video_each + h)],
+                peer_at,
+                count - 1,
             )
         )
-    for b in range(blocks_each):
-        results.append(
-            (
-                lambda peer, b=b: mixed_a.at[b, peer],
-                lambda source, b=b: audio_out.at[:, column(source * blocks_each + b)],
-            )
-        )
-    ways = streams + results
+    ways.append(
+        (
+            lambda peer: mixed_a.at[peer % half],
+            lambda source: audio_out.at[:, columns(source % half)],
+            peer_near,
+            half - 1,
+        )
+    )
 
     def outgoing(k, peer):
         return pltpu.make_async_remote_copy(
@@ -338,7 +367,7 @@
             device_id_type=pl.DeviceIdType.MESH,
         )
 
-    for k in range(len(streams)):
+    for k in range(first):
         kept(k).start()
     pl.semaphore_wait(barrier, count - 1)
 
@@ -354,13 +383,13 @@
         for j, array, near in near_pairs:
             near_copy(2 + j, array, near, 2, me - 1).start()
 
-    for k in range(len(streams)):
+    for k in range(first):
 
         def send(t, carry, k=k):
-            outgoing(k, peer_at(t)).start()
+            outgoing(k, ways[k][2](t)).start()
             return carry
 
-        lax.fori_loop(0, count - 1, send, 0)
+        lax.fori_loop(0, ways[k][3], send, 0)
 
     @pl.when(me == 0)
     def _():
@@ -391,9 +420,9 @@
     inside = (bounds[0:1, :] <= tile) & (tile < bounds[1:2, :])
     inside = jnp.where(inside, 1.0, 0.0).astype(jnp.bfloat16)
     seen = []
-    for side in range(3):
+    for slot in range(3):
         stretch = lax.broadcasted_iota(jnp.int32, (spans, audio_rows), 1) // STRETCH_LEN
-        stretch = stretch + (me + side - 1) * (audio_rows // STRETCH_LEN)
+        stretch = stretch + (me + slot - 1) * (audio_rows // STRETCH_LEN)
         picks = stretch == lax.broadcasted_iota(jnp.int32, (spans, audio_rows), 0)
         picks = jnp.where(picks, 1.0, 0.0).astype(jnp.bfloat16)
         part = jnp.dot(inside, picks, preferred_element_type=jnp.float32)
@@ -403,25 +432,25 @@
         lanes = slice(b * LANES, (b + 1) * LANES)
         stacked = lane_heads(local_cq[:, lanes])
         scores = []
-        for side in range(3):
+        for slot in range(3):
             part = lax.dot_general(
                 stacked,
-                near_k[side, :, lanes],
+                near_k[slot, :, lanes],
                 (((1,), (1,)), ((), ())),
                 preferred_element_type=jnp.float32,
             )
-            scores.append(jnp.where(seen[side] > 0.5, part, jnp.float32(-1e30)))
+            scores.append(jnp.where(seen[slot] > 0.5, part, jnp.float32(-1e30)))
         peak = jnp.max(jnp.maximum(jnp.maximum(scores[0], scores[1]), scores[2]), axis=1, keepdims=True)
         factor = jnp.float32(audio_scaling * math.log2(math.e))
         weights = [jnp.exp2((part - peak) * factor) for part in scores]
         summed = jnp.sum(weights[0] + weights[1] + weights[2], axis=1, keepdims=True)
         mixed = sum(
             jnp.dot(
-                weights[side].astype(jnp.bfloat16),
-                near_v[side, :, lanes],
+                weights[slot].astype(jnp.bfloat16),
+                near_v[slot, :, lanes],
                 preferred_element_type=jnp.float32,
             )
-            for side in range(3)
+            for slot in range(3)
         )
         mixed_c[:, lanes] = merge_lane_heads(mixed / summed, rows).astype(jnp.bfloat16)
 
@@ -429,58 +458,116 @@
         kept(k).wait()
 
         def one(t, carry):
-            incoming(k, peer_at(t)).wait_recv()
+            incoming(k, ways[k][2](t)).wait_recv()
             return carry
 
-        lax.fori_loop(0, count - 1, one, 0)
-
-    def run_blocks(k, mix):
+        lax.fori_loop(0, ways[k][3], one, 0)
+
+    def run_blocks(k, steps, mix):
         def one(t, carry):
-            mix(peer_at(t))
+            mix(ways[k][2](t))
 
             @pl.when(t > 0)
             def _():
-                outgoing(k, peer_at(t - 1)).start()
+                outgoing(k, ways[k][2](t - 1)).start()
 
             return carry
 
-        lax.fori_loop(0, count, one, 0)
-
-    first = len(streams)
+        lax.fori_loop(0, steps, one, 0)
+        kept(k).start()
+
+    def part_copy(j, array, land):
+        return pltpu.make_async_remote_copy(
+            src_ref=array,
+            dst_ref=land,
+            send_sem=part_send.at[j],
+            recv_sem=part_recv.at[j],
+            device_id=device((me + half) % count),
+            device_id_type=pl.DeviceIdType.MESH,
+        )
+
+    part_copies = [part_copy(0, far_part, got_part), part_copy(1, far_stat, got_stat)]
+    stat_lane = lax.broadcasted_iota(jnp.int32, (audio_rows, LANES), 1)
+    each = LANES // AUDIO_DIM
+
+    def audio_parts(first_source, part, stat):
+        def one(j, stats):
+            queries = land_aq[first_source + j]
+            for b in range(blocks_each):
+                lanes = slice(b * LANES, (b + 1) * LANES)
+                mixed, peak, summed = softmax_mix(
+                    lane_heads(queries[:, lanes]), land_ck[:, lanes], land_cv[:, lanes], audio_scaling
+                )
+                part[j, :, lanes] = merge_lane_heads(mixed, audio_rows).astype(part.dtype)
+                level = peak * jnp.float32(audio_scaling * math.log2(math.e)) + jnp.log2(summed)
+                for i in range(each):
+                    stats = jnp.where(
+                        stat_lane == (j * blocks_each + b) * each + i,
+                        level[i * audio_rows : (i + 1) * audio_rows],
+                        stats,
+                    )
+            return stats
+
+        stat[...] = lax.fori_loop(0, half, one, jnp.zeros((audio_rows, LANES), jnp.float32))
+
+    def merge_parts(peer):
+        j = peer % half
+        for b in range(blocks_each):
+            lanes = slice(b * LANES, (b + 1) * LANES)
+            shares = []
+            for i in range(each):
+                picked = stat_lane == (j * blocks_each + b) * each + i
+                mine = jnp.sum(jnp.where(picked, own_stat[...], 0.0), axis=1, keepdims=True)
+                other = jnp.sum(jnp.where(picked, got_stat[...], 0.0), axis=1, keepdims=True)
+                peak = jnp.maximum(mine, other)
+                mine = jnp.exp2(mine - peak)
+                other = jnp.exp2(other - peak)
+                total = mine + other
+                shares.append((mine / total, other / total))
+            own_share, got_share = (
+                merge_lane_heads(
+                    jnp.concatenate(
+                        [jnp.broadcast_to(s[w], (audio_rows, LANES)) for s in shares], axis=0
+                    ),
+                    audio_rows,
+                )
+                for w in range(2)
+            )
+            merged = own_part[j, :, lanes] * own_share
+            merged = merged + got_part[j, :, lanes].astype(jnp.float32) * got_share
+            mixed_a[j, :, lanes] = merged.astype(jnp.bfloat16)
+
     for h in range(video_each):
-        for k in range(3 * h, 3 * h + 3):
+        for k in video_ways[h]:
             await_stream(k)
 
         def mix_video(source, h=h):
-            mixed = softmax_mix(land_q[h, row(source), :], land_k[h], land_v[h], video_scaling)
+            mixed, peak, summed = softmax_mix(
+                land_q[h, row(source), :], land_k[h], land_v[h], video_scaling
+            )
             mixed_v[h, row(source), :] = mixed.astype(jnp.bfloat16)
 
-        run_blocks(first + h, mix_video)
+        run_blocks(first + h, count, mix_video)
         if h == 0:
             finished = pltpu.make_async_copy(mixed_c, video_cross, local_sem.at[0])
             finished.start()
-    for b in range(blocks_each):
-        base = 3 * video_each + 3 * b
-        for k in range(base, base + 3):
-            await_stream(k)
-
-        def mix_audio(source, b=b):
-            mixed = softmax_mix(
-                lane_heads(land_aq[b, source]), land_ck[b], land_cv[b], audio_scaling
-            )
-            mixed_a[b, source] = merge_lane_heads(mixed, audio_rows).astype(jnp.bfloat16)
-
-        run_blocks(first + video_each + b, mix_audio)
-    for k in range(first, len(ways)):
-        kept(k).start()
+            for k in audio_ways:
+                await_stream(k)
+            audio_parts((1 - side) * half, far_part, far_stat)
+            audio_parts(side * half, own_part, own_stat)
+            for copy in part_copies:
+                copy.start()
+    for copy in part_copies:
+        copy.wait()
+    run_blocks(len(ways) - 1, half, merge_parts)
 
     for k in range(len(ways)):
 
         def sent(t, carry, k=k):
-            outgoing(k, peer_at(t)).wait_send()
+            outgoing(k, ways[k][2](t)).wait_send()
             return carry
 
-        lax.fori_loop(0, count - 1, sent, 0)
+        lax.fori_loop(0, ways[k][3], sent, 0)
     for k in range(first, len(ways)):
         await_stream(k)
     finished.wait()
@@ -501,8 +588,9 @@
     rows = vid_q.shape[0]
     audio_rows = aud_q.shape[0]
     video_each = vid_q.shape[1] // HEAD_DIM // count
-    blocks_each = aud_q.shape[1] // LANES // count
-    kinds = 4 * video_each + 4 * blocks_each
+    halves = count // 2
+    width = aud_q.shape[1] // halves
+    kinds = 4 * video_each + 4
     half = jnp.bfloat16
     place = pl.BlockSpec(memory_space=pl.ANY)
     return pl.pallas_call(
@@ -518,11 +606,17 @@
             pltpu.VMEM((video_each, count * rows, HEAD_DIM), half),
             pltpu.VMEM((video_each, count * rows, HEAD_DIM), half),
             pltpu.VMEM((video_each, count * rows, HEAD_DIM), half),
-            pltpu.VMEM((blocks_each, count, audio_rows, LANES), half),
-            pltpu.VMEM((blocks_each, count * rows, LANES), half),
-            pltpu.VMEM((blocks_each, count * rows, LANES), half),
+            pltpu.VMEM((count, audio_rows, width), half),
+            pltpu.VMEM((halves * rows, width), half),
+            pltpu.VMEM((halves * rows, width), half),
             pltpu.VMEM((video_each, count * rows, HEAD_DIM), half),
-            pltpu.VMEM((blocks_each, count, audio_rows, LANES), half),
+            pltpu.VMEM((halves, audio_rows, width), half),
+            pltpu.VMEM((halves, audio_rows, width), jnp.float32),
+            pltpu.VMEM((audio_rows, LANES), jnp.float32),
+            pltpu.VMEM((halves, audio_rows, width), half),
+            pltpu.VMEM((audio_rows, LANES), jnp.float32),
+            pltpu.VMEM((halves, audio_rows, width), half),
+            pltpu.VMEM((audio_rows, LANES), jnp.float32),
             pltpu.VMEM((3, audio_rows, aud_k.shape[1]), half),
             pltpu.VMEM((3, audio_rows, aud_k.shape[1]), half),
             pltpu.VMEM(cross_q.shape, half),
@@ -531,6 +625,8 @@
             pltpu.SemaphoreType.DMA((kinds, count)),
             pltpu.SemaphoreType.DMA((4,)),
             pltpu.SemaphoreType.DMA((4,)),
+            pltpu.SemaphoreType.DMA((2,)),
+            pltpu.SemaphoreType.DMA((2,)),
             pltpu.SemaphoreType.DMA((3,)),
         ],
         compiler_params=pltpu.CompilerParams(collective_id=0, has_side_effects=True),
@@ -542,8 +638,9 @@
     sub_count = lax.axis_size("sub")
     count = lax.axis_size("seq") * sub_count
     video_heads = arrays[0].shape[1] // HEAD_DIM
-    audio_blocks = arrays[3].shape[1] // LANES
-    if video_heads % count == 0 and audio_blocks % count == 0:
+    audio_heads = arrays[3].shape[1] // AUDIO_DIM
+    halved = lax.axis_size("seq") % 2 == 0 and audio_heads <= LANES
+    if halved and video_heads % count == 0 and audio_heads % count == 0:
         return exchanged_body(count, sub_count, *arrays)
     return gathered_body(*arrays)
 

time: 88.8 us -> 80.1 us (0.902)
  Pallas kernels: 84.6 us -> 75.9 us
    pallas_call x1, Pallas kernels: 84.6 us -> 75.9 us  [exchanged_body(): pl.pallas_call(partial(exchange_kernel, count, sub_count), out_shape=(jax...]
where the time goes in v2:
time: 80.1 us; the launch traced here: 79.9 us
  Pallas kernels  75.9 us (95%)
  local copies, waits for them, and re-layouts  3.4 us (4%)
    pallas_call x1, Pallas kernels, exchanged_body(): pl.pallas_call(partial(exchange_kernel, count, sub_count), out_shape=(jax...  75.9 us
    unnamed x7, local copies, waits for them, and re-layouts  3.4 us

profile of v2, /device:TPU:0, one launch (start us, length us, event | category | flops | bytes accessed | tf_op | source)
XLA Modules:
  0.0 79.9 jit_solution(4690798364157121721)
XLA Ops:
  0.6 75.9 %joint_attention.1 = (bf16[160,2048]{1,0:T(8,128)(2,1)}, bf16[40,1024]{1,0:T(8,128)(2,1)}, bf16[160,1024]{1,0:T(8,128)(2,1)}) custom-call(bf16[160,2048]{1,0:T(8,128)(2,1)} %vid_q.1, bf16[160,2048]{1,0:T(8,128)(2,1)} %vid_k.1, bf16[160,2048]{1,0:T(8,128)(2,1)} %vid_v.1, bf16[40,1024]{1,0:T(8,128)(2,1)} %aud_q.1, bf16[160,1024]{1,0:T(8,128)(2,1)} %cross_k.1, ...), custom_call_target="tpu_custom_call" | custom-call | tf_op jit(solution)/shard_map/joint_attention/pallas_call | solution.py:596
  76.5 0.0 copy-start.1
  76.5 0.0 copy-start
  76.5 2.0 %copy.16 = bf16[160,2048]{1,0:T(8,128)(2,1)} copy(bf16[160,2048]{1,0:T(8,128)(2,1)} %get-tuple-element.6) | data formatting | bytes 1310720
  78.6 0.0 copy-done.1
  78.6 0.6 copy.17
  79.2 0.0 copy-done
  79.2 0.7 copy.18
Async XLA Ops:
  76.5 2.1 %copy-start.1 = (bf16[40,1024]{1,0:T(8,128)(2,1)S(1)}, bf16[40,1024]{1,0:T(8,128)(2,1)}, u32[]{:S(2)}) copy-start(bf16[40,1024]{1,0:T(8,128)(2,1)} %get-tuple-element.7) | copy-start | bytes 245764
  76.5 2.7 %copy-start = (bf16[160,1024]{1,0:T(8,128)(2,1)S(1)}, bf16[160,1024]{1,0:T(8,128)(2,1)}, u32[]{:S(2)}) copy-start(bf16[160,1024]{1,0:T(8,128)(2,1)} %get-tuple-element.8) | copy-start | bytes 983044

commit v3 on v2

--- a/solution.py
+++ b/solution.py
@@ -223,7 +223,6 @@
     near_k,
     near_v,
     local_cq,
-    mixed_c,
     send_sem,
     recv_sem,
     near_send,
@@ -249,7 +248,7 @@
         return {"seq": peer // sub_count, "sub": peer % sub_count}
 
     def peer_at(t):
-        return (me + half + (1 - 2 * (t % 2)) * ((t + 1) // 2)) % count
+        return ((side + 1 - t // half) % 2) * half + (place + t + t // half) % half
 
     def peer_near(t):
         return side * half + (place + 1 + t) % half
@@ -452,7 +451,7 @@
             )
             for slot in range(3)
         )
-        mixed_c[:, lanes] = merge_lane_heads(mixed / summed, rows).astype(jnp.bfloat16)
+        video_cross[:, lanes] = merge_lane_heads(mixed / summed, rows).astype(jnp.bfloat16)
 
     def await_stream(k):
         kept(k).wait()
@@ -549,8 +548,6 @@
 
         run_blocks(first + h, count, mix_video)
         if h == 0:
-            finished = pltpu.make_async_copy(mixed_c, video_cross, local_sem.at[0])
-            finished.start()
             for k in audio_ways:
                 await_stream(k)
             audio_parts((1 - side) * half, far_part, far_stat)
@@ -570,7 +567,6 @@
         lax.fori_loop(0, ways[k][3], sent, 0)
     for k in range(first, len(ways)):
         await_stream(k)
-    finished.wait()
 
     @pl.when(me < count - 1)
     def _():
@@ -581,6 +577,14 @@
     def _():
         for j, array, near in near_pairs:
             near_copy(2 + j, array, near, 2, me - 1).wait_send()
+
+
+def store_kernel(*refs):
+    copies = [pltpu.make_async_copy(refs[i], refs[3 + i], refs[6].at[i]) for i in range(3)]
+    for copy in copies:
+        copy.start()
+    for copy in copies:
+        copy.wait()
 
 
 def exchanged_body(count, sub_count, *arrays):
@@ -593,15 +597,11 @@
     kinds = 4 * video_each + 4
     half = jnp.bfloat16
     place = pl.BlockSpec(memory_space=pl.ANY)
-    return pl.pallas_call(
+    held = pl.pallas_call(
         partial(exchange_kernel, count, sub_count),
-        out_shape=(
-            jax.ShapeDtypeStruct(vid_q.shape, half),
-            jax.ShapeDtypeStruct(aud_q.shape, half),
-            jax.ShapeDtypeStruct(cross_q.shape, half),
-        ),
+        out_shape=tuple(pltpu.VMEM(a.shape, half) for a in (vid_q, aud_q, cross_q)),
         in_specs=[place] * 9 + [pl.BlockSpec(memory_space=pltpu.VMEM)],
-        out_specs=(place, place, place),
+        out_specs=(pl.BlockSpec(memory_space=pltpu.VMEM),) * 3,
         scratch_shapes=[
             pltpu.VMEM((video_each, count * rows, HEAD_DIM), half),
             pltpu.VMEM((video_each, count * rows, HEAD_DIM), half),
@@ -620,7 +620,6 @@
             pltpu.VMEM((3, audio_rows, aud_k.shape[1]), half),
             pltpu.VMEM((3, audio_rows, aud_k.shape[1]), half),
             pltpu.VMEM(cross_q.shape, half),
-            pltpu.VMEM(cross_q.shape, half),
             pltpu.SemaphoreType.DMA((kinds, count)),
             pltpu.SemaphoreType.DMA((kinds, count)),
             pltpu.SemaphoreType.DMA((4,)),
@@ -632,6 +631,14 @@
         compiler_params=pltpu.CompilerParams(collective_id=0, has_side_effects=True),
         name="joint_attention",
     )(*arrays)
+    return pl.pallas_call(
+        store_kernel,
+        out_shape=tuple(jax.ShapeDtypeStruct(a.shape, half) for a in (vid_q, aud_q, cross_q)),
+        in_specs=[pl.BlockSpec(memory_space=pltpu.VMEM)] * 3,
+        out_specs=(place, place, place),
+        scratch_shapes=[pltpu.SemaphoreType.DMA((3,))],
+        name="store_results",
+    )(*[pltpu.with_memory_space_constraint(x, pltpu.VMEM) for x in held])
 
 
 def body(*arrays):

time: 80.1 us -> 77.6 us (0.969)
  local copies, waits for them, and re-layouts: 3.4 us -> 0 us
  Pallas kernels: 75.9 us -> 76.8 us
    unnamed x7 -> x0, local copies, waits for them, and re-layouts: 3.4 us -> none
    pallas_call x1 -> x2, Pallas kernels: 75.9 us -> 76.8 us  [the longest x1 75.8 us: exchanged_body(): pl.pallas_call(partial(exchange_kernel, count, sub_count), out_shape=tupl...]
where the time goes in v3:
time: 77.6 us; the launch traced here: 77.4 us
  Pallas kernels  76.8 us (99%)
    pallas_call x1, Pallas kernels, exchanged_body(): pl.pallas_call(partial(exchange_kernel, count, sub_count), out_shape=tupl...  75.8 us

profile of v3, /device:TPU:0, one launch (start us, length us, event | category | flops | bytes accessed | tf_op | source)
XLA Modules:
  0.0 77.4 jit_solution(9126786979577299142)
XLA Ops:
  0.6 75.8 %joint_attention.1 = (bf16[160,2048]{1,0:T(8,128)(2,1)S(1)}, bf16[40,1024]{1,0:T(8,128)(2,1)S(1)}, bf16[160,1024]{1,0:T(8,128)(2,1)S(1)}) custom-call(bf16[160,2048]{1,0:T(8,128)(2,1)} %vid_q.1, bf16[160,2048]{1,0:T(8,128)(2,1)} %vid_k.1, bf16[160,2048]{1,0:T(8,128)(2,1)} %vid_v.1, bf16[40,1024]{1,0:T(8,128)(2,1)} %aud_q.1, bf16[160,1024]{1,0:T(8,128)(2,1)} %cross_k.1, ...), custom_call_target="tpu_custom_call" | custom-call | tf_op jit(solution)/shard_map/joint_attention/pallas_call | solution.py:600
  76.5 1.0 %store_results.1 = (bf16[160,2048]{1,0:T(8,128)(2,1)}, bf16[40,1024]{1,0:T(8,128)(2,1)}, bf16[160,1024]{1,0:T(8,128)(2,1)}) custom-call(bf16[160,2048]{1,0:T(8,128)(2,1)S(1)} %get-tuple-element.6.refs_0_, bf16[40,1024]{1,0:T(8,128)(2,1)S(1)} %get-tuple-element.7.refs_1_, bf16[160,1024]{1,0:T(8,128)(2,1)S(1)} %get-tuple-element.8.refs_2_), custom_call_target="tpu_custom_call" | custom-call | tf_op jit(solution)/shard_map/store_results/pallas_call | solution.py:634

commit v4 on v3

--- a/solution.py
+++ b/solution.py
@@ -507,17 +507,25 @@
                     )
             return stats
 
-        stat[...] = lax.fori_loop(0, half, one, jnp.zeros((audio_rows, LANES), jnp.float32))
+        stats = lax.fori_loop(0, half, one, jnp.zeros((audio_rows, LANES), jnp.float32))
+        padded = jnp.concatenate(
+            [stats, jnp.zeros((LANES - audio_rows, LANES), jnp.float32)], axis=0
+        )
+        stat[...] = padded.T[: stat.shape[0]]
 
     def merge_parts(peer):
         j = peer % half
+        unpacked = []
+        for stat in (own_stat, got_stat):
+            rest = jnp.zeros((LANES - stat.shape[0], LANES), jnp.float32)
+            unpacked.append(jnp.concatenate([stat[...], rest], axis=0).T[:audio_rows])
         for b in range(blocks_each):
             lanes = slice(b * LANES, (b + 1) * LANES)
             shares = []
             for i in range(each):
                 picked = stat_lane == (j * blocks_each + b) * each + i
-                mine = jnp.sum(jnp.where(picked, own_stat[...], 0.0), axis=1, keepdims=True)
-                other = jnp.sum(jnp.where(picked, got_stat[...], 0.0), axis=1, keepdims=True)
+                mine = jnp.sum(jnp.where(picked, unpacked[0], 0.0), axis=1, keepdims=True)
+                other = jnp.sum(jnp.where(picked, unpacked[1], 0.0), axis=1, keepdims=True)
                 peak = jnp.maximum(mine, other)
                 mine = jnp.exp2(mine - peak)
                 other = jnp.exp2(other - peak)
@@ -595,6 +603,7 @@
     halves = count // 2
     width = aud_q.shape[1] // halves
     kinds = 4 * video_each + 4
+    levels = -(-aud_q.shape[1] // AUDIO_DIM // 8) * 8
     half = jnp.bfloat16
     place = pl.BlockSpec(memory_space=pl.ANY)
     held = pl.pallas_call(
@@ -612,11 +621,11 @@
             pltpu.VMEM((video_each, count * rows, HEAD_DIM), half),
             pltpu.VMEM((halves, audio_rows, width), half),
             pltpu.VMEM((halves, audio_rows, width), jnp.float32),
-            pltpu.VMEM((audio_rows, LANES), jnp.float32),
+            pltpu.VMEM((levels, LANES), jnp.float32),
             pltpu.VMEM((halves, audio_rows, width), half),
-            pltpu.VMEM((audio_rows, LANES), jnp.float32),
+            pltpu.VMEM((levels, LANES), jnp.float32),
             pltpu.VMEM((halves, audio_rows, width), half),
-            pltpu.VMEM((audio_rows, LANES), jnp.float32),
+            pltpu.VMEM((levels, LANES), jnp.float32),
             pltpu.VMEM((3, audio_rows, aud_k.shape[1]), half),
             pltpu.VMEM((3, audio_rows, aud_k.shape[1]), half),
             pltpu.VMEM(cross_q.shape, half),
@@ -646,7 +655,7 @@
     count = lax.axis_size("seq") * sub_count
     video_heads = arrays[0].shape[1] // HEAD_DIM
     audio_heads = arrays[3].shape[1] // AUDIO_DIM
-    halved = lax.axis_size("seq") % 2 == 0 and audio_heads <= LANES
+    halved = lax.axis_size("seq") % 2 == 0 and max(audio_heads, arrays[3].shape[0]) <= LANES
     if halved and video_heads % count == 0 and audio_heads % count == 0:
         return exchanged_body(count, sub_count, *arrays)
     return gathered_body(*arrays)

time: 77.6 us -> 77.3 us (level)
  no operation moved by 1% of the time
where the time goes in v4:
time: 77.3 us; the launch traced here: 77.1 us
  Pallas kernels  76.5 us (99%)
    pallas_call x1, Pallas kernels, exchanged_body(): pl.pallas_call(partial(exchange_kernel, count, sub_count), out_shape=tupl...  75.5 us

profile of v4, /device:TPU:0, one launch (start us, length us, event | category | flops | bytes accessed | tf_op | source)
XLA Modules:
  0.0 77.1 jit_solution(12822417099595450051)
XLA Ops:
  0.6 75.5 %joint_attention.1 = (bf16[160,2048]{1,0:T(8,128)(2,1)S(1)}, bf16[40,1024]{1,0:T(8,128)(2,1)S(1)}, bf16[160,1024]{1,0:T(8,128)(2,1)S(1)}) custom-call(bf16[160,2048]{1,0:T(8,128)(2,1)} %vid_q.1, bf16[160,2048]{1,0:T(8,128)(2,1)} %vid_k.1, bf16[160,2048]{1,0:T(8,128)(2,1)} %vid_v.1, bf16[40,1024]{1,0:T(8,128)(2,1)} %aud_q.1, bf16[160,1024]{1,0:T(8,128)(2,1)} %cross_k.1, ...), custom_call_target="tpu_custom_call" | custom-call | tf_op jit(solution)/shard_map/joint_attention/pallas_call | solution.py:609
  76.1 1.0 %store_results.1 = (bf16[160,2048]{1,0:T(8,128)(2,1)}, bf16[40,1024]{1,0:T(8,128)(2,1)}, bf16[160,1024]{1,0:T(8,128)(2,1)}) custom-call(bf16[160,2048]{1,0:T(8,128)(2,1)S(1)} %get-tuple-element.6.refs_0_, bf16[40,1024]{1,0:T(8,128)(2,1)S(1)} %get-tuple-element.7.refs_1_, bf16[160,1024]{1,0:T(8,128)(2,1)S(1)} %get-tuple-element.8.refs_2_), custom_call_target="tpu_custom_call" | custom-call | tf_op jit(solution)/shard_map/store_results/pallas_call | solution.py:643
